TPU v7x, 512 devices: a whole 4x4x16 slice. The times are simulated.
512 devices in a mesh: row: 16 (over z), col: 32 (over y, x, core).
Axes of the slice: x: 4, y: 4, z: 16, core: 2. Of those that a mesh axis runs over, the one named last changes fastest.
Arguments:
- tokens: bfloat16 [2048, 8192], P('row'), may hold values from -6 to 6
- gate_weight: bfloat16 [8192, 16384], P('row', 'col'), may hold values from -0.09375 to 0.09375
- up_weight: bfloat16 [8192, 16384], P('row', 'col'), may hold values from -0.09375 to 0.09375
- down_weight: bfloat16 [16384, 8192], P('col', 'row'), may hold values from -0.0625 to 0.0625
- gate_mask: int32 [64, 128], P('row', 'col'), may hold values from 0 to 1, as said below
- up_mask: int32 [64, 128], P('row', 'col'), may hold values from 0 to 1, as said below
- down_mask: int32 [128, 64], P('col', 'row'), may hold values 0 or 1
Outputs:
- mixed: bfloat16 [2048, 8192], P('col', 'row')
Inputs may be any that keep to these rules, and one draw needn't show every extreme that they name: `gate_mask`: each device's block of 4 x 4 tiles keeps between 4 and 12 tiles; in each column of devices some block keeps exactly 12. `up_mask`: as for gate_mask, drawn independently.
All inputs are finite; a program needn't handle non-finite values. No bound on the sum of `down_mask` on one device may be relied on, other than what follows from the above.
Results may differ from a plain program's by a relative error of at most 0.02.
Values may be sent and summed in bfloat16 or wider, within the bound.
A program may use at most 128 MiB of HBM per device.

v0:
```python
import jax
import jax.numpy as jnp
from jax import lax
from jax.sharding import PartitionSpec as P


def expand(weight, mask):
    rows, cols = weight.shape
    tile_rows, tile_cols = mask.shape
    tile = rows // tile_rows
    shaped = weight.reshape(tile_rows, tile, tile_cols, tile)
    return (shaped * mask.astype(weight.dtype)[:, None, :, None]).reshape(rows, cols)


def pack_tiles(weight, mask):
    rows, cols = weight.shape
    tile_rows, tile_cols = mask.shape
    tile = rows // tile_rows
    count = tile_rows * tile_cols
    slots = 3 * count // 4
    tiles = (
        weight.reshape(tile_rows, tile, tile_cols, tile)
        .transpose(0, 2, 1, 3)
        .reshape(count, tile * tile)
    )
    flags = mask.reshape(count)
    place = jnp.cumsum(flags) - 1
    chosen = (place[None, :] == jnp.arange(slots, dtype=jnp.int32)[:, None]) & (flags[None, :] == 1)
    packed = jnp.dot(chosen.astype(jnp.bfloat16), tiles, preferred_element_type=jnp.float32)
    packed = packed.astype(jnp.bfloat16).reshape(slots, tile, tile)
    where_from = jnp.sum(jnp.where(chosen, jnp.arange(count, dtype=jnp.int32)[None, :], 0), axis=1)
    return (packed, where_from)


def unpack_tiles(packed, where_from, groups, tile_rows, tile_cols):
    slots, tile = (packed.shape[0] // groups, packed.shape[1])
    count = tile_rows * tile_cols
    packed = packed.reshape(groups, slots, tile, tile)
    where_from = where_from.reshape(groups, slots)
    spread = (where_from[:, None, :] == jnp.arange(count, dtype=jnp.int32)[None, :, None]).astype(
        jnp.bfloat16
    )
    dense = jnp.einsum("gcs,gsab->gcab", spread, packed, preferred_element_type=jnp.float32).astype(
        jnp.bfloat16
    )
    dense = dense.reshape(groups, tile_rows, tile_cols, tile, tile).transpose(0, 1, 3, 2, 4)
    return dense.reshape(groups, tile_rows * tile, tile_cols * tile)


def on_device(tokens, gate_weight, up_weight, down_weight, gate_mask, up_mask, down_mask):
    tok_rows = tokens.shape[0]
    panel_rows, panel_cols = gate_weight.shape
    tile_rows, tile_cols = gate_mask.shape
    slots = 3 * tile_rows * tile_cols // 4
    gate_packed, gate_from = pack_tiles(gate_weight, gate_mask)
    up_packed, up_from = pack_tiles(up_weight, up_mask)
    gate_piece = lax.all_gather(gate_packed, "row", axis=0, tiled=True)
    up_piece = lax.all_gather(up_packed, "row", axis=0, tiled=True)
    gate_where = lax.all_gather(gate_from, "row", axis=0, tiled=True)
    up_where = lax.all_gather(up_from, "row", axis=0, tiled=True)
    groups = gate_piece.shape[0] // slots
    columns = tokens
    columns = columns.reshape(tok_rows, groups, panel_rows)

    def partial_value(piece, where_from):
        dense = unpack_tiles(piece, where_from, groups, tile_rows, tile_cols)
        product = jnp.einsum("tgr,grc->gtc", columns, dense, preferred_element_type=jnp.float32)
        rounded = lax.optimization_barrier(product.astype(jnp.bfloat16)).astype(jnp.float32)
        return jnp.sum(rounded, axis=0)

    gate = partial_value(gate_piece, gate_where)
    up = partial_value(up_piece, up_where)
    hidden = (jax.nn.silu(gate) * up).astype(jnp.bfloat16)
    all_hidden = lax.all_gather(hidden, "row", axis=0, tiled=True)
    down_eff = expand(down_weight, down_mask)
    return lax.psum_scatter(
        jnp.dot(all_hidden, down_eff, preferred_element_type=jnp.float32).astype(jnp.bfloat16),
        "col",
        scatter_dimension=0,
        tiled=True,
    )


def solution(mesh):
    return jax.shard_map(
        on_device,
        mesh=mesh,
        in_specs=(
            P("row", None),
            P("row", "col"),
            P("row", "col"),
            P("col", "row"),
            P("row", "col"),
            P("row", "col"),
            P("col", "row"),
        ),
        out_specs=P("col", "row"),
        check_vma=False,
    )
```

profile of v0, /device:TPU:2, one launch (start us, length us, event | category | flops | bytes accessed | tf_op | source)
XLA Modules:
  0.0 405.5 jit_solution(13095400725307765612)
XLA Ops:
  6.5 0.8 reshape.148
  7.3 0.7 broadcast_compare_fusion.1
  8.0 0.1 add_reduce_fusion.1
  8.1 0.1 eq.82
  8.2 1.2 reshape.122
  9.4 0.1 copy.33
  9.5 0.4 convolution_convert_fusion.1
  9.9 0.1 copy.48
  10.0 0.8 slice
  10.8 0.0 all-gather.4.cloned.1.call-update
  10.8 0.0 all-gather.6.cloned.1.call-start
  10.9 0.8 reshape.149
  11.6 0.7 broadcast_compare_fusion
  12.3 0.1 eq.91
  12.4 1.2 reshape.130
  13.6 0.1 copy.38
  13.7 0.1 add_reduce_fusion
  13.8 0.4 convolution_convert_fusion
  14.3 0.1 copy.50
  14.4 0.8 slice.1
  15.2 0.0 all-gather.6.cloned.1.call-update
  15.2 0.0 all-gather.8.cloned.1.call-start
  15.2 1.3 dynamic-slice
  17.2 0.1 select_reduce_fusion.1
  17.3 0.2 dynamic-update-slice
  17.5 0.1 select_reduce_fusion
  17.6 0.2 dynamic-update-slice.1
  17.9 26.8 %all-reduce.2 = (s32[192]{0:T(256)S(1)}, s32[192]{0:T(256)S(1)}) all-reduce(s32[192]{0:T(256)S(1)} %dynamic-update-slice.1, s32[192]{0:T(256)S(1)} %dynamic-update-slice), channel_id=1, replica_groups=mesh['row'=16,'col'=32] {'row'}, use_global_device_ids=true, to_apply=%add.1 | all-reduce | flops 384 | bytes 3072
  44.7 0.1 eq.83
  44.8 0.1 eq.92
  44.9 56.9 %all-gather.4.cloned.1.call-done = bf16[192,128,128]{2,1,0:T(8,128)(2,1)} async-done(((bf16[12,128,128]{2,1,0:T(8,128)(2,1)}), bf16[192,128,128]{2,1,0:T(8,128)(2,1)}) %all-gather.4.cloned.1.call-update) | async-done | bytes 6291472 | tf_op jit(solution)/shard_map/all_gather | solution.py:57
  101.7 10.4 %fusion.4 = bf16[16,16,128,128]{3,1,2,0:T(8,128)(2,1)} fusion(bf16[16,12,128,128]{3,2,1,0:T(8,128)(2,1)} %bitcast.65, s32[16,12]{1,0:T(8,128)S(1)} %eq.83), kind=kOutput, calls=%fused_computation.7 | convolution fusion | flops 104860672 | bytes 14680832 | tf_op jit(solution)/shard_map/gcs,gsab->gcab/dot_general | solution.py:43
  112.1 15.4 %copy.35 = bf16[16,4,128,4,128]{2,1,4,3,0:T(4,128)(2,1)} copy(bf16[16,4,128,4,128]{4,3,1,2,0:T(4,128)(2,1)} %bitcast.62) | data formatting | bytes 16777216 | tf_op jit(solution)/shard_map/transpose | solution.py:46
  127.6 13.2 %reshape.127 = bf16[16,512,512]{1,2,0:T(8,128)(2,1)} reshape(bf16[16,4,128,4,128]{2,1,4,3,0:T(4,128)(2,1)} %copy.35) | data formatting | bytes 16777216 | tf_op jit(solution)/shard_map/reshape | solution.py:47
  140.7 6.4 %convert_bitcast_fusion.1 = bf16[16,128,512]{1,2,0:T(8,128)(2,1)S(1)} fusion(bf16[16,512,512]{1,2,0:T(8,128)(2,1)} %reshape.127, bf16[16,16,8,512]{3,2,1,0:T(8,128)(2,1)} %bitcast.74), kind=kOutput, calls=%fused_computation.17 | convolution fusion | flops 1074790400 | bytes 12582912 | tf_op jit(solution)/shard_map/tgr,grc->gtc/dot_general | solution.py:67
  147.2 39.8 %all-gather.6.cloned.1.call-done = bf16[192,128,128]{2,1,0:T(8,128)(2,1)} async-done(((bf16[12,128,128]{2,1,0:T(8,128)(2,1)}), bf16[192,128,128]{2,1,0:T(8,128)(2,1)}) %all-gather.6.cloned.1.call-update) | async-done | bytes 6291472 | tf_op jit(solution)/shard_map/all_gather | solution.py:58
  186.9 7.2 %fusion.7 = bf16[16,16,128,128]{3,1,2,0:T(8,128)(2,1)S(1)} fusion(bf16[16,12,128,128]{3,2,1,0:T(8,128)(2,1)} %bitcast.66, s32[16,12]{1,0:T(8,128)S(1)} %eq.92), kind=kOutput, calls=%fused_computation.8 | convolution fusion | flops 104860672 | bytes 14680832 | tf_op jit(solution)/shard_map/gcs,gsab->gcab/dot_general | solution.py:43
  194.1 5.8 %copy.81 = bf16[16,4,4,128,128]{4,2,3,1,0:T(4,128)(2,1)} copy(bf16[16,4,4,128,128]{4,2,1,3,0:T(4,128)(2,1)S(1)} %bitcast.63) | data formatting | bytes 16777216 | tf_op jit(solution)/shard_map/reshape | solution.py:46
  200.0 13.1 %reshape.135 = bf16[16,512,512]{2,1,0:T(8,128)(2,1)} reshape(bf16[16,4,128,4,128]{4,3,2,1,0:T(4,128)(2,1)} %bitcast.64) | data formatting | bytes 16777216 | tf_op jit(solution)/shard_map/reshape | solution.py:47
  213.1 6.6 %convert_bitcast_fusion = bf16[16,128,512]{1,2,0:T(8,128)(2,1)S(1)} fusion(bf16[16,512,512]{2,1,0:T(8,128)(2,1)} %reshape.135, bf16[16,16,8,512]{3,2,1,0:T(8,128)(2,1)} %bitcast.75), kind=kOutput, calls=%fused_computation.16 | convolution fusion | flops 1074790400 | bytes 12582912 | tf_op jit(solution)/shard_map/tgr,grc->gtc/dot_general | solution.py:67
  219.6 0.6 convert_reduce_fusion
  220.2 0.7 multiply_convert_fusion
  220.9 0.0 all-gather.8.cloned.1.call-update
  220.9 0.0 reduce-scatter.2.cloned.1.call-start
  221.0 75.3 %all-gather.8.cloned.1.call-done = bf16[2048,512]{0,1:T(8,128)(2,1)} async-done(((bf16[128,512]{0,1:T(8,128)(2,1)}), bf16[2048,512]{0,1:T(8,128)(2,1)}) %all-gather.8.cloned.1.call-update) | async-done | bytes 2097168 | tf_op jit(solution)/shard_map/all_gather | solution.py:74
  296.3 0.2 mul.20
  296.6 4.2 %convolution_convert_fusion.2 = bf16[2048,512]{1,0:T(8,128)(2,1)} fusion(bf16[2048,512]{0,1:T(8,128)(2,1)} %all-gather.8.cloned.1.call-done, bf16[512,512]{1,0:T(8,128)(2,1)S(1)} %copy-done.1, bf16[64,8,4,128]{3,2,1,0:T(4,128)(2,1)S(1)} %bitcast.73), kind=kOutput, calls=%fused_computation.11 | convolution fusion | flops 1075052544 | bytes 5242880 | tf_op jit(solution)/shard_map/dot_general | solution.py:77
  300.8 98.1 %reduce-scatter.2.cloned.1.call-done = bf16[64,512]{1,0:T(8,128)(2,1)} async-done(((bf16[2048,512]{1,0:T(8,128)(2,1)}), bf16[64,512]{1,0:T(8,128)(2,1)}) %reduce-scatter.2.cloned.1.call-update) | async-done | bytes 65552 | tf_op jit(solution)/shard_map/reduce_scatter | solution.py:76
  (11 shorter events, 0.1 us)
Async XLA Ops:
  6.5 95.2 %all-gather.4.cloned.1.call-start = ((), (), s32[]{:S(2)}) async-start(), calls=%async_computation.1 | async-start | bytes 6684672 | tf_op jit(solution)/shard_map/all_gather | solution.py:57
  10.8 176.1 %all-gather.6.cloned.1.call-start = ((), (), s32[]{:S(2)}) async-start(), calls=%async_computation.2 | async-start | bytes 6684672 | tf_op jit(solution)/shard_map/all_gather | solution.py:58
  15.2 281.1 %all-gather.8.cloned.1.call-start = ((), (), s32[]{:S(2)}) async-start(), calls=%async_computation.3 | async-start | bytes 2228224 | tf_op jit(solution)/shard_map/all_gather | solution.py:74
  213.1 7.9 %copy-start = (s32[4,4]{1,0:T(4,128)S(1)}, s32[4,4]{1,0:T(4,128)}, u32[]{:S(2)}) copy-start(s32[4,4]{1,0:T(4,128)} %param.13) | copy-start | bytes 196
  213.1 83.5 %copy-start.1 = (bf16[512,512]{1,0:T(8,128)(2,1)S(1)}, bf16[512,512]{1,0:T(8,128)(2,1)}, u32[]{:S(2)}) copy-start(bf16[512,512]{1,0:T(8,128)(2,1)} %param.10) | copy-start | bytes 1572868
  220.9 178.0 %reduce-scatter.2.cloned.1.call-start = ((), (), s32[]{:S(2)}) async-start(), calls=%async_computation.4 | async-start | bytes 2162688 | tf_op jit(solution)/shard_map/reduce_scatter | solution.py:76
Sparse Core Ops, SparseCore 0:
  11.0 90.7 all-gather.3
  103.8 83.0 all-gather.5
  221.1 75.2 all-gather.7
  300.9 97.9 reduce-scatter.1
where the time goes:
time: 407 us; the launch traced here: 405 us
  waiting for transfers between devices  270 us (66%)
  local copies, waits for them, and re-layouts  55.7 us (14%)
  matrix products  35.5 us (9%)
  blocking collectives  26.8 us (7%)
  between operations  13.9 us (3%)
    reduce_scatter x1, waiting for transfers between devices, on_device(): lax.psum_scatter(jnp.dot(all_hidden, down_eff, preferred_element_type=jnp...  98.1 us
    all_gather x1, waiting for transfers between devices, on_device(): all_hidden = lax.all_gather(hidden, 'row', axis=0, tiled=True)  75.3 us
    all_gather x1, waiting for transfers between devices, on_device(): gate_piece = lax.all_gather(gate_packed, 'row', axis=0, tiled=True)  56.9 us
    all_gather x1, waiting for transfers between devices, on_device(): up_piece = lax.all_gather(up_packed, 'row', axis=0, tiled=True)  39.8 us
    unnamed x1, blocking collectives  26.8 us
    reshape x2, local copies, waits for them, and re-layouts, unpack_tiles(): return dense.reshape(groups, tile_rows * tile, tile_cols * tile)  26.3 us
    dot_general x2, matrix products, unpack_tiles(): jnp.einsum('gcs,gsab->gcab', spread, packed, preferred_element_type=jnp.f...  17.6 us
    transpose x1, local copies, waits for them, and re-layouts, unpack_tiles(): dense.reshape(groups, tile_rows, tile_cols, tile, tile)  15.4 us
  transfers between devices with their start and end apart: 4, of which 4 were waited for; matrix products, arithmetic and copies ran while one was open for 13% of the time, Pallas kernels for 0%

commit v1 on v0

--- a/solution.py
+++ b/solution.py
@@ -54,7 +54,10 @@
     slots = 3 * tile_rows * tile_cols // 4
     gate_packed, gate_from = pack_tiles(gate_weight, gate_mask)
     up_packed, up_from = pack_tiles(up_weight, up_mask)
-    gate_piece = lax.all_gather(gate_packed, "row", axis=0, tiled=True)
+    count_2 = lax.axis_size("row")
+    blocks = jnp.stack([gate_packed for _ in range(count_2)])
+    blocks = lax.all_to_all(blocks, "row", split_axis=0, concat_axis=0)
+    gate_piece = jnp.concatenate(blocks, axis=0)
     up_piece = lax.all_gather(up_packed, "row", axis=0, tiled=True)
     gate_where = lax.all_gather(gate_from, "row", axis=0, tiled=True)
     up_where = lax.all_gather(up_from, "row", axis=0, tiled=True)

time: 407 us -> 644 us (1.58)
  blocking collectives: 26.8 us -> 342 us
  waiting for transfers between devices: 270 us -> 176 us
  starting transfers between devices: 0.13 us -> 15.5 us
    unnamed x1, blocking collectives: 26.8 us -> 342 us
    all_gather x1 -> x0, waiting for transfers between devices: 56.9 us -> none  [on_device(): gate_piece = lax.all_gather(gate_packed, 'row', axis=0, tiled=True)]
    all_gather x1, waiting for transfers between devices: 39.8 us -> 0.02 us  [on_device(): up_piece = lax.all_gather(up_packed, 'row', axis=0, tiled=True)]
    all_to_all x0 -> x1, starting transfers between devices: none -> 15.4 us  [on_device(): blocks = lax.all_to_all(blocks, 'row', split_axis=0, concat_axis=0)]
  transfers between devices with their start and end apart: 4 -> 4, of which waited for: 4 -> 2; matrix products, arithmetic and copies ran while one was open for 13% -> 6% of each run, Pallas kernels for 0% -> 0%
where the time goes in v1:
time: 644 us; the launch traced here: 642 us
  blocking collectives  342 us (53%)
  waiting for transfers between devices  176 us (27%)
  local copies, waits for them, and re-layouts  57.4 us (9%)
  matrix products  35.4 us (5%)
  starting transfers between devices  15.5 us (2%)
  between operations  13.9 us (2%)
    unnamed x1, blocking collectives  342 us
    reduce_scatter x1, waiting for transfers between devices, on_device(): lax.psum_scatter(jnp.dot(all_hidden, down_eff, preferred_element_type=jnp...  98.1 us
    all_gather x1, waiting for transfers between devices, on_device(): all_hidden = lax.all_gather(hidden, 'row', axis=0, tiled=True)  77.3 us
    reshape x2, local copies, waits for them, and re-layouts, unpack_tiles(): return dense.reshape(groups, tile_rows * tile, tile_cols * tile)  26.2 us
    dot_general x2, matrix products, unpack_tiles(): jnp.einsum('gcs,gsab->gcab', spread, packed, preferred_element_type=jnp.f...  17.6 us
    all_to_all x1, starting transfers between devices, on_device(): blocks = lax.all_to_all(blocks, 'row', split_axis=0, concat_axis=0)  15.4 us
    transpose x1, local copies, waits for them, and re-layouts, unpack_tiles(): dense.reshape(groups, tile_rows, tile_cols, tile, tile)  15.3 us
  transfers between devices with their start and end apart: 4, of which 2 were waited for; matrix products, arithmetic and copies ran while one was open for 6% of the time, Pallas kernels for 0%

profile of v1, /device:TPU:2, one launch (start us, length us, event | category | flops | bytes accessed | tf_op | source)
XLA Modules:
  0.0 642.5 jit_solution(8966633429543696483)
XLA Ops:
  6.5 0.8 reshape.142
  7.3 0.7 broadcast_compare_fusion.1
  8.0 0.1 add_reduce_fusion.1
  8.1 0.1 eq.82
  8.2 1.2 reshape.118
  9.4 0.1 copy.34
  9.5 0.4 convolution_convert_fusion.1
  9.9 0.1 copy.49
  10.0 4.2 stack.3
  14.3 15.4 %all-to-all-start = ((bf16[16,12,128,128]{3,2,1,0:T(8,128)(2,1)}), bf16[16,12,128,128]{3,2,1,0:T(8,128)(2,1)}, u32[]{:S(2)}, u32[]{:S(2)}) async-start(bf16[16,12,128,128]{3,2,1,0:T(8,128)(2,1)} %stack.3), calls=%async_computation | async-start | bytes 12582912 | tf_op jit(solution)/shard_map/all_to_all | solution.py:59
  29.7 0.0 all-gather.3.cloned.1.call-start
  29.7 0.1 reshape.143
  29.8 0.1 eq.91
  29.9 0.1 reshape.124
  30.0 0.1 copy.39
  30.2 0.1 add_reduce_fusion
  30.3 0.4 convolution_convert_fusion
  30.7 0.1 copy.51
  30.8 0.8 slice.1
  31.6 0.0 all-gather.3.cloned.1.call-update
  31.6 0.0 all-gather.5.cloned.1.call-start
  31.7 1.3 dynamic-slice
  33.6 0.1 select_reduce_fusion.1
  33.7 0.2 dynamic-update-slice
  34.0 0.1 select_reduce_fusion
  34.1 0.2 dynamic-update-slice.1
  34.3 342.1 %all-reduce.2 = (s32[192]{0:T(256)S(1)}, s32[192]{0:T(256)S(1)}) all-reduce(s32[192]{0:T(256)S(1)} %dynamic-update-slice.1, s32[192]{0:T(256)S(1)} %dynamic-update-slice), channel_id=1, replica_groups=mesh['row'=16,'col'=32] {'row'}, use_global_device_ids=true, to_apply=%add.1 | all-reduce | flops 384 | bytes 3072
  376.4 0.1 eq.83
  376.5 0.1 eq.92
  376.6 0.0 all-gather.3.cloned.1.call-done
  376.6 7.2 %fusion.7 = bf16[16,16,128,128]{3,1,2,0:T(8,128)(2,1)S(1)} fusion(bf16[16,12,128,128]{3,2,1,0:T(8,128)(2,1)} %bitcast.64, s32[16,12]{1,0:T(8,128)S(1)} %eq.92), kind=kOutput, calls=%fused_computation.8 | convolution fusion | flops 104860672 | bytes 14680832 | tf_op jit(solution)/shard_map/gcs,gsab->gcab/dot_general | solution.py:43
  383.8 6.0 copy.82
  389.8 13.1 %reshape.129 = bf16[16,512,512]{2,1,0:T(8,128)(2,1)} reshape(bf16[16,4,128,4,128]{4,3,2,1,0:T(4,128)(2,1)} %bitcast.63) | data formatting | bytes 16777216 | tf_op jit(solution)/shard_map/reshape | solution.py:47
  402.9 6.5 %convert_bitcast_fusion = bf16[16,128,512]{1,2,0:T(8,128)(2,1)S(1)} fusion(bf16[16,512,512]{2,1,0:T(8,128)(2,1)} %reshape.129, bf16[16,16,8,512]{3,2,1,0:T(8,128)(2,1)} %bitcast.72), kind=kOutput, calls=%fused_computation.16 | convolution fusion | flops 1074790400 | bytes 12582912 | tf_op jit(solution)/shard_map/tgr,grc->gtc/dot_general | solution.py:70
  409.4 0.0 all-to-all-done
  409.4 10.4 %fusion.4 = bf16[16,16,128,128]{3,1,2,0:T(8,128)(2,1)} fusion(bf16[16,12,128,128]{3,2,1,0:T(8,128)(2,1)} %all-to-all-done, s32[16,12]{1,0:T(8,128)S(1)} %eq.83), kind=kOutput, calls=%fused_computation.7 | convolution fusion | flops 104860672 | bytes 14680832 | tf_op jit(solution)/shard_map/gcs,gsab->gcab/dot_general | solution.py:43
  419.8 15.3 %copy.36 = bf16[16,4,128,4,128]{2,1,4,3,0:T(4,128)(2,1)} copy(bf16[16,4,128,4,128]{4,3,1,2,0:T(4,128)(2,1)} %bitcast.62) | data formatting | bytes 16777216 | tf_op jit(solution)/shard_map/transpose | solution.py:46
  435.1 13.1 %reshape.121 = bf16[16,512,512]{1,2,0:T(8,128)(2,1)} reshape(bf16[16,4,128,4,128]{2,1,4,3,0:T(4,128)(2,1)} %copy.36) | data formatting | bytes 16777216 | tf_op jit(solution)/shard_map/reshape | solution.py:47
  448.2 6.4 convert_bitcast_fusion.1
  454.6 0.6 convert_reduce_fusion
  455.2 0.7 multiply_convert_fusion
  455.9 0.0 all-gather.5.cloned.1.call-update
  455.9 0.0 reduce-scatter.2.cloned.1.call-start
  456.0 77.3 %all-gather.5.cloned.1.call-done = bf16[2048,512]{0,1:T(8,128)(2,1)} async-done(((bf16[128,512]{0,1:T(8,128)(2,1)}), bf16[2048,512]{0,1:T(8,128)(2,1)}) %all-gather.5.cloned.1.call-update) | async-done | bytes 2097168 | tf_op jit(solution)/shard_map/all_gather | solution.py:77
  533.3 0.2 mul.20
  533.6 4.2 convolution_convert_fusion.2
  537.8 0.0 reduce-scatter.2.cloned.1.call-update
  537.8 98.1 %reduce-scatter.2.cloned.1.call-done = bf16[64,512]{1,0:T(8,128)(2,1)} async-done(((bf16[2048,512]{1,0:T(8,128)(2,1)}), bf16[64,512]{1,0:T(8,128)(2,1)}) %reduce-scatter.2.cloned.1.call-update) | async-done | bytes 65552 | tf_op jit(solution)/shard_map/reduce_scatter | solution.py:79
  (15 shorter events, 0.1 us)
Async XLA Ops:
  14.3 15.4 %copy-start.1 = (s32[4,4]{1,0:T(4,128)S(1)}, s32[4,4]{1,0:T(4,128)}, u32[]{:S(2)}) copy-start(s32[4,4]{1,0:T(4,128)} %param.12) | copy-start | bytes 196
  14.3 15.6 %copy-start = (bf16[512,512]{1,0:T(8,128)(2,1)S(1)}, bf16[512,512]{1,0:T(8,128)(2,1)}, u32[]{:S(2)}) copy-start(bf16[512,512]{1,0:T(8,128)(2,1)} %param.9) | copy-start | bytes 1572868
  14.3 395.1 %all-to-all-start = ((bf16[16,12,128,128]{3,2,1,0:T(8,128)(2,1)}), bf16[16,12,128,128]{3,2,1,0:T(8,128)(2,1)}, u32[]{:S(2)}, u32[]{:S(2)}) async-start(bf16[16,12,128,128]{3,2,1,0:T(8,128)(2,1)} %stack.3), calls=%async_computation | async-start | bytes 12582912 | tf_op jit(solution)/shard_map/all_to_all | solution.py:59
  29.7 346.9 %all-gather.3.cloned.1.call-start = ((), (), s32[]{:S(2)}) async-start(), calls=%async_computation.2 | async-start | bytes 6684672 | tf_op jit(solution)/shard_map/all_gather | solution.py:61
  31.6 501.7 %all-gather.5.cloned.1.call-start = ((), (), s32[]{:S(2)}) async-start(), calls=%async_computation.3 | async-start | bytes 2228224 | tf_op jit(solution)/shard_map/all_gather | solution.py:77
  448.2 7.8 %copy-start.2 = (s32[4,4]{1,0:T(4,128)S(1)}, s32[4,4]{1,0:T(4,128)}, u32[]{:S(2)}) copy-start(s32[4,4]{1,0:T(4,128)} %param.13) | copy-start | bytes 196
  448.2 85.3 %copy-start.3 = (bf16[512,512]{1,0:T(8,128)(2,1)S(1)}, bf16[512,512]{1,0:T(8,128)(2,1)}, u32[]{:S(2)}) copy-start(bf16[512,512]{1,0:T(8,128)(2,1)} %param.10) | copy-start | bytes 1572868
  455.9 180.0 %reduce-scatter.2.cloned.1.call-start = ((), (), s32[]{:S(2)}) async-start(), calls=%async_computation.4 | async-start | bytes 2162688 | tf_op jit(solution)/shard_map/reduce_scatter | solution.py:79
Sparse Core Ops, SparseCore 0:
  32.6 334.4 all-gather.2
  456.1 77.2 all-gather.4
  537.9 97.9 reduce-scatter.1
